TPU v7x, 32 devices: a whole 2x2x4 slice. The times are simulated.
32 devices in a mesh: case: 2 (over x), ax: 16 (over z, y, core).
Axes of the slice: x: 2, y: 2, z: 4, core: 2. Of those that a mesh axis runs over, the one named last changes fastest.
Arguments:
- populations: float32 [19, 32, 128, 128], P(None, 'ax', 'case'), parts along dimension 2, may hold values from 0 to 1, as said below
- solid_mask: int32 [32, 128, 128], P('ax', 'case'), parts along dimension 1, may hold values from 0 to 1, as said below
- link_flags: int32 [2, 32, 128, 128], P(None, 'ax', 'case'), parts along dimension 2, may hold values from 0 to 511, as said below
- inlet_cells: int32 [1024], P('case'), parts along dimension 0, may hold values from 0 to 8191, as said below
- pod_basis: float32 [512, 3, 512], P(None, None, 'ax'), may hold values from -0.15625 to 0.15625
- mri_frames: float32 [24, 6, 512], P(None, 'case', 'ax'), parts along dimension 1
- frame_index: int32 [1], replicated, may hold values from 0 to 23
Outputs:
- advanced_populations: float32 [19, 32, 128, 128], P(None, 'ax', 'case'), parts along dimension 2
- inflow: float32 [2, 6, 512], P(None, 'case', 'ax'), parts along dimension 1
There are 2 independent parts, one for each index of `case`. A program takes and returns all parts, laid end to end along the dimension named above; an argument that names none is the same for every part. Nothing has to cross between parts.
Inputs may be any that keep to these rules, and one draw needn't show every extreme that they name: `solid_mask`: 1 marks a wall cell, 0 a fluid cell; the two outermost rows and columns of every cross-section are wall cells. `link_flags`: at a fluid cell, bit (i - 1) mod 9 of word (i - 1) div 9 is set exactly when the cell at minus c_i is a wall cell, the grid being continued past its first and last plane by repeating those planes; zero at wall cells. `inlet_cells`: distinct cells of the first plane, all of them fluid cells. `populations`: every entry is positive.
All inputs are finite; a program needn't handle non-finite values.
Results may differ from a plain program's by a relative error of at most 0.00011.
Values sent between devices are 32-bit elements; how exact they have to be, the bound alone decides.
A program may use at most 64 MiB of HBM per device.

v0:
```python
import math
import jax
import jax.numpy as jnp
from jax import lax
from jax.sharding import PartitionSpec as P

STEPS = 2
lattice_c = (
    (0, 0, 0),
    (1, 0, 0),
    (-1, 0, 0),
    (0, 1, 0),
    (0, -1, 0),
    (0, 0, 1),
    (0, 0, -1),
    (1, 1, 0),
    (-1, -1, 0),
    (1, -1, 0),
    (-1, 1, 0),
    (1, 0, 1),
    (-1, 0, -1),
    (1, 0, -1),
    (-1, 0, 1),
    (0, 1, 1),
    (0, -1, -1),
    (0, 1, -1),
    (0, -1, 1),
)
lattice_w = (1.0 / 3.0,) + (1.0 / 18.0,) * 6 + (1.0 / 36.0,) * 12
opposite_of = (0, 2, 1, 4, 3, 6, 5, 8, 7, 10, 9, 12, 11, 14, 13, 16, 15, 18, 17)
pair_list = ((0, 0), (1, 1), (2, 2), (0, 1), (0, 2), (1, 2))
relax_base = 0.52
smagorinsky_sq = 0.04
inflow_scale = 0.05


def extended(array, sides, width):
    for axis, dim in sides:
        count, length = (lax.axis_size(axis), array.shape[dim])
        up = [(i, (i + 1) % count) for i in range(count - 1)]
        down = [(j, i) for i, j in up]
        last = lax.slice_in_dim(array, length - width, length, axis=dim)
        leading = lax.slice_in_dim(array, 0, width, axis=dim)
        before = lax.ppermute(last, axis, up)
        after = lax.ppermute(leading, axis, down)
        array = jnp.concatenate([before, array, after], axis=dim)
    return array


def moment_rows():
    listed = [[1.0] * 19]
    for axis_a in range(3):
        listed.append([float(vector[axis_a]) for vector in lattice_c])
    for pair_a, pair_b in pair_list:
        listed.append([float(vector[pair_a] * vector[pair_b]) for vector in lattice_c])
    return jnp.asarray(listed, dtype=jnp.float32)


def equilibrium(density, velocity):
    lattice = jnp.asarray(
        [[float(entry) for entry in vector] for vector in lattice_c], dtype=jnp.float32
    )
    weights = jnp.asarray(list(lattice_w), dtype=jnp.float32).reshape((19,) + (1,) * density.ndim)
    projected = jnp.einsum("iq,q...->i...", lattice, velocity, precision=lax.Precision.HIGHEST)
    speed_sq = jnp.sum(velocity * velocity, axis=0)
    return (
        weights
        * density[None]
        * (1.0 + 3.0 * projected + 4.5 * projected * projected - 1.5 * speed_sq[None])
    )


def collide(populations, solid_mask):
    moments = jnp.einsum(
        "mi,i...->m...", moment_rows(), populations, precision=lax.Precision.HIGHEST
    )
    density = moments[0]
    velocity = moments[1:4] / density[None]
    nonequil = populations - equilibrium(density, velocity)
    stress = jnp.einsum(
        "mi,i...->m...", moment_rows()[4:], nonequil, precision=lax.Precision.HIGHEST
    )
    magnitude = stress[0] * stress[0] + stress[1] * stress[1] + stress[2] * stress[2]
    magnitude = magnitude + 2.0 * (
        stress[3] * stress[3] + stress[4] * stress[4] + stress[5] * stress[5]
    )
    relax_time = 0.5 * (
        relax_base
        + jnp.sqrt(
            relax_base * relax_base
            + 18.0 * math.sqrt(2.0) * smagorinsky_sq * jnp.sqrt(magnitude) / density
        )
    )
    relaxed = populations - nonequil / relax_time[None]
    return jnp.where(solid_mask[None] == 1, populations, relaxed)


def stream(relaxed, ghost_low, ghost_high, link_flags, solid_mask):
    padded = jnp.concatenate([ghost_low[:, None], relaxed, ghost_high[:, None]], axis=1)
    planes_here = relaxed.shape[1]
    read = []
    for direction in range(19):
        step_x, step_y, step_z = lattice_c[direction]
        source = padded[direction, 1 - step_z : 1 - step_z + planes_here]
        source = jnp.roll(source, (step_y, step_x), axis=(1, 2))
        if direction > 0:
            word = link_flags[(direction - 1) // 9]
            linked = jnp.bitwise_and(jnp.right_shift(word, (direction - 1) % 9), 1)
            source = jnp.where(linked == 1, relaxed[opposite_of[direction]], source)
        read.append(jnp.where(solid_mask == 1, relaxed[direction], source))
    return jnp.stack(read)


def inlet_plane(speeds, inlet_cells, height, plane_width):
    inlet_speed = jnp.zeros((3, height * plane_width), jnp.float32).at[:, inlet_cells].set(speeds)
    inlet_speed = inlet_speed.reshape(3, height, plane_width)
    return equilibrium(jnp.ones((height, plane_width), jnp.float32), inlet_speed)


def neighbour_planes(relaxed):
    padded = extended(relaxed, (("ax", 1),), 1)
    ghost_low = padded[:, 0]
    ghost_high = padded[:, -1]
    return (ghost_low, ghost_high)


def body(populations, solid_mask, link_flags, inlet_cells, pod_basis, mri_frames, frame_index):
    frames_total = mri_frames.shape[0]
    frame_slot = lax.broadcasted_iota(jnp.int32, (STEPS, frames_total), 1)
    segment_slot = lax.broadcasted_iota(jnp.int32, (STEPS, frames_total), 0)
    selector = (frame_slot == (frame_index[0] + segment_slot) % frames_total).astype(jnp.float32)
    chosen = jnp.einsum("sf,fjc->sjc", selector, mri_frames, precision=lax.Precision.HIGHEST)
    partial_terms = jnp.einsum("kjc,sjc->sk", pod_basis, chosen, precision=lax.Precision.HIGHEST)
    coefficients = lax.psum(partial_terms, "ax")
    local_inflow = jnp.einsum(
        "kjc,sk->sjc", pod_basis, coefficients, precision=lax.Precision.HIGHEST
    )
    whole_inflow = lax.all_gather(local_inflow, "ax", axis=2, tiled=True)
    position = lax.axis_index("ax")
    axis_count = lax.axis_size("ax")
    height = populations.shape[2]
    plane_width = populations.shape[3]
    for segment_index in range(STEPS):
        relaxed = collide(populations, solid_mask)
        inlet_ghost = inlet_plane(
            inflow_scale * whole_inflow[segment_index], inlet_cells, height, plane_width
        )
        ghost_low, ghost_high = neighbour_planes(relaxed)
        ghost_low = jnp.where(position == 0, inlet_ghost, ghost_low)
        ghost_high = jnp.where(position == axis_count - 1, relaxed[:, -1], ghost_high)
        populations = stream(relaxed, ghost_low, ghost_high, link_flags, solid_mask)
    return (populations, local_inflow)


def solution(mesh):
    in_specs = (
        P(None, "ax", "case", None),
        P("ax", "case", None),
        P(None, "ax", "case", None),
        P("case"),
        P(None, None, "ax"),
        P(None, "case", "ax"),
        P(),
    )
    out_specs = (P(None, "ax", "case", None), P(None, "case", "ax"))
    return jax.shard_map(body, mesh=mesh, in_specs=in_specs, out_specs=out_specs, check_vma=False)
```

profile of v0, /device:TPU:1, one launch (start us, length us, event | category | flops | bytes accessed | tf_op | source)
XLA Modules:
  0.0 146.1 jit_solution(2449302820524212767)
XLA Ops:
  0.6 0.9 broadcast_compare_fusion
  1.6 3.0 %fusion.4 = f32[10,2,64,128]{3,0,2,1:T(8,128)S(1)} fusion(f32[10,19,1,1]{1,0,3,2:T(8,128)} %constant.81, f32[19,2,64,128]{3,2,1,0:T(8,128)} %param.19), kind=kOutput, calls=%fused_computation.12 | convolution fusion | flops 37355520 | bytes 1901304 | tf_op jit(solution)/shard_map/mi,i...->m.../dot_general | solution.py:74
  4.9 1.5 %fusion.149 = f32[19,2,64,128]{3,0,2,1:T(8,128)S(1)} fusion(f32[19,3,1,1]{0,1,3,2:T(4,128)S(1)} %copy-done.22, f32[10,2,64,128]{3,0,2,1:T(8,128)S(1)} %fusion.4, f32[2,64,128]{2,1,0:T(8,128)S(1)} %bitcast.600), kind=kOutput, calls=%fused_computation.338 | convolution fusion | flops 11255808 | bytes 1574912 | tf_op jit(solution)/shard_map/iq,q...->i.../dot_general | solution.py:64
  6.8 0.8 copy-done.3
  7.7 2.8 %copy_subtract_fusion = f32[19,2,64,128]{3,0,2,1:T(8,128)S(1)} fusion(f32[19,2,64,128]{3,2,1,0:T(8,128)S(1)} %copy-done.3, f32[19,2,64,128]{3,2,1,0:T(8,128)S(1)} %get-tuple-element.100, f32[19,2,64,128]{3,2,1,0:T(8,128)S(1)} %get-tuple-element.61, f32[19,2,64,128]{3,0,2,1:T(8,128)S(1)} %fusion.149, f32[19,2,64,128]{3,2,1,0:T(8,128)S(1)} %get-tuple-element.60, ...), kind=kLoop, calls=%fused_computation.11 | loop fusion | flops 1556480 | bytes 7536640 | tf_op jit(solution)/shard_map/sub | solution.py:79
  10.5 0.9 fusion.171
  11.9 1.0 subtract_select_fusion
  13.1 0.9 copy-done.5
  14.1 2.1 %collective-permute-start.1 = (f32[19,1,64,128]{3,2,1,0:T(8,128)S(1)}, f32[19,1,64,128]{3,2,1,0:T(8,128)}, u32[]{:S(2)}, u32[]{:S(2)}) collective-permute-start(f32[19,1,64,128]{3,2,1,0:T(8,128)S(1)} %slice.827), channel_id=1, source_target_pairs={{1,0},{2,1},{3,2},{4,3},{5,4},{6,5},{7,6},{8,7},{9,8},{10,9},{11,1... | collective-permute-start | bytes 1867784 | tf_op jit(solution)/shard_map/ppermute | solution.py:45
  18.0 31.4 %psum.7 = f32[2,512]{1,0:T(2,128)S(1)} all-reduce(f32[2,512]{1,0:T(2,128)S(1)} %convolution_bitcast_fusion), channel_id=1, replica_groups=mesh['case'=2,'ax'=16] {'ax'}, use_global_device_ids=true, to_apply=%region_1.2 | all-reduce | flops 1024 | bytes 8192 | tf_op jit(solution)/shard_map/psum | solution.py:134
  49.3 1.0 fusion.139
  50.9 0.8 copy.150
  51.7 23.9 %all_gather.3 = f32[2,3,512]{1,0,2:T(2,128)S(1)} all-gather(f32[2,3,32]{1,0,2:T(2,128)S(1)} %copy.150), channel_id=1, replica_groups=mesh['case'=2,'ax'=16] {'ax'}, dimensions={2}, use_global_device_ids=true | all-gather | bytes 13056 | tf_op jit(solution)/shard_map/all_gather | solution.py:138
  75.6 1.4 slice_multiply_fusion
  79.0 4.3 %scatter_custom_fusion = f32[3,8192]{0,1:T(8,128)} fusion(s32[512]{0:T(512)} %compare_select_fusion, f32[512,3]{1,0:T(8,128)} %bitcast.636, f32[]{:T(128)} %constant.31.clone.1), kind=kCustom, calls=%fused_computation.7 | custom fusion | bytes 98816 | tf_op jit(solution)/shard_map/scatter | solution.py:115
  83.4 3.4 %multiply_reduce_fusion.1 = f32[8192]{0:T(1024)S(1)} fusion(f32[3,8192]{0,1:T(8,128)} %scatter_custom_fusion), kind=kLoop, calls=%fused_computation.3 | loop fusion | flops 40960 | bytes 131072 | tf_op jit(solution)/shard_map/reduce_sum | solution.py:65
  88.6 4.3 %scatter_custom_fusion.1 = f32[3,8192]{0,1:T(8,128)} fusion(s32[512]{0:T(512)} %compare_select_fusion, f32[512,3]{1,0:T(8,128)} %bitcast.635, f32[]{:T(128)} %constant.31.clone.1), kind=kCustom, calls=%fused_computation.5 | custom fusion | bytes 98816 | tf_op jit(solution)/shard_map/scatter | solution.py:115
  92.9 3.5 %multiply_reduce_fusion = f32[8192]{0:T(1024)S(1)} fusion(f32[3,8192]{0,1:T(8,128)} %scatter_custom_fusion.1), kind=kLoop, calls=%fused_computation.2 | loop fusion | flops 40960 | bytes 131072 | tf_op jit(solution)/shard_map/reduce_sum | solution.py:65
  96.4 4.6 %fusion.172 = f32[19,64,128]{2,0,1:T(8,128)} fusion(f32[19,3,1]{0,1,2:T(4,128)S(1)} %copy-done.24, f32[3,64,128]{0,2,1:T(8,128)S(1)} %bitcast.598), kind=kOutput, calls=%fused_computation.343 | convolution fusion | flops 5603328 | bytes 721124 | tf_op jit(solution)/shard_map/iq,q...->i.../dot_general | solution.py:64
  101.0 2.0 %bitcast_select_fusion = (f32[19,1,64,128]{3,2,1,0:T(8,128)S(1)}, f32[19,1,64,128]{3,2,1,0:T(8,128)}) fusion(f32[19,1,64,128]{3,2,1,0:T(8,128)} %collective-permute-done.1, pred[]{:T(512)S(6)} %eq.197, f32[19,2,64,128]{3,2,1,0:T(8,128)S(1)} %copy.143), kind=kLoop, calls=%fused_computation.45 | loop fusion | flops 155648 | bytes 2490369 | tf_op jit(solution)/shard_map/jit(_where)/select_n | solution.py:150
  103.1 3.9 %collective-permute-start = (f32[19,1,64,128]{3,2,1,0:T(8,128)}, f32[19,1,64,128]{3,2,1,0:T(8,128)}, u32[]{:S(2)}, u32[]{:S(2)}) collective-permute-start(f32[19,1,64,128]{3,2,1,0:T(8,128)} %get-tuple-element.80), channel_id=1, source_target_pairs={{0,1},{1,2},{2,3},{3,4},{4,5},{5,6},{6,7},{7,8},{8,9},{9,10},{10,1... | collective-permute-start | bytes 1867784 | tf_op jit(solution)/shard_map/ppermute | solution.py:44
  107.0 1.7 %slice.867 = f32[1,2,64,128]{3,0,2,1:T(1,128)} slice(f32[19,2,64,128]{3,0,2,1:T(8,128)} %copy-done.5), slice={[18:19], [0:2], [0:64], [0:128]} | slice | bytes 131072 | tf_op jit(solution)/shard_map/slice | solution.py:109
  110.0 0.9 constant_dynamic-update-slice_fusion.14
  110.9 5.6 %fusion.173 = f32[19,64,128]{2,0,1:T(8,128)S(1)} fusion(f32[19,3,1]{0,1,2:T(4,128)} %constant.84, f32[3,64,128]{0,2,1:T(8,128)} %bitcast.597), kind=kOutput, calls=%fused_computation.344 | convolution fusion | flops 5603328 | bytes 721124 | tf_op jit(solution)/shard_map/iq,q...->i.../dot_general | solution.py:64
  116.5 1.3 fusion.19
  120.2 1.7 %fusion.8 = f32[10,2,64,128]{3,0,2,1:T(8,128)S(1)} fusion(f32[10,19,1,1]{1,0,3,2:T(8,128)S(1)} %copy-done.19, f32[19,2,64,128]{3,2,1,0:T(8,128)S(1)} %get-tuple-element.2), kind=kOutput, calls=%fused_computation.16 | convolution fusion | flops 37355520 | bytes 1901304 | tf_op jit(solution)/shard_map/mi,i...->m.../dot_general | solution.py:74
  122.2 1.5 %fusion.150 = f32[19,2,64,128]{3,0,2,1:T(8,128)S(1)} fusion(f32[19,3,1,1]{0,1,3,2:T(4,128)S(1)} %copy-done.23, f32[10,2,64,128]{3,0,2,1:T(8,128)S(1)} %fusion.8, f32[2,64,128]{2,1,0:T(8,128)S(1)} %bitcast.604), kind=kOutput, calls=%fused_computation.339 | convolution fusion | flops 11255808 | bytes 1574912 | tf_op jit(solution)/shard_map/iq,q...->i.../dot_general | solution.py:64
  124.4 1.6 %fusion.6 = f32[6,2,64,128]{3,0,2,1:T(8,128)S(1)} fusion(f32[6,19,1,1]{1,0,3,2:T(8,128)S(1)} %copy-done.21, f32[19,2,64,128]{3,2,1,0:T(8,128)S(1)} %fusion.14), kind=kOutput, calls=%fused_computation.14 | convolution fusion | flops 22413312 | bytes 1638856 | tf_op jit(solution)/shard_map/mi,i...->m.../dot_general | solution.py:80
  126.8 2.3 %collective-permute-start.2 = (f32[19,1,64,128]{3,2,0,1:T(8,128)S(1)}, f32[19,1,64,128]{3,2,0,1:T(8,128)S(1)}, u32[]{:S(2)}, u32[]{:S(2)}) collective-permute-start(f32[19,1,64,128]{3,2,0,1:T(8,128)S(1)} %get-tuple-element.67), channel_id=1, source_target_pairs={{0,1},{1,2},{2,3},{3,4},{4,5},{5,6},{6,7},{7,8},{8,9},{9,10},{10,1... | collective-permute-start | bytes 1867784 | tf_op jit(solution)/shard_map/ppermute | solution.py:44
  129.6 2.1 %collective-permute-start.3 = (f32[19,1,64,128]{3,2,0,1:T(8,128)S(1)}, f32[19,1,64,128]{3,2,0,1:T(8,128)S(1)}, u32[]{:S(2)}, u32[]{:S(2)}) collective-permute-start(f32[19,1,64,128]{3,2,0,1:T(8,128)S(1)} %get-tuple-element.66), channel_id=1, source_target_pairs={{1,0},{2,1},{3,2},{4,3},{5,4},{6,5},{7,6},{8,7},{9,8},{10,9},{11,1... | collective-permute-start | bytes 1867784 | tf_op jit(solution)/shard_map/ppermute | solution.py:45
  131.7 11.2 %collective-permute-done.2 = f32[19,1,64,128]{3,2,0,1:T(8,128)S(1)} collective-permute-done((f32[19,1,64,128]{3,2,0,1:T(8,128)S(1)}, f32[19,1,64,128]{3,2,0,1:T(8,128)S(1)}, u32[]{:S(2)}, u32[]{:S(2)}) %collective-permute-start.2) | collective-permute-done | bytes 622624 | tf_op jit(solution)/shard_map/ppermute | solution.py:44
  145.1 1.0 copy-done.27
  (172 shorter events, 14.6 us)
Async XLA Ops:
  0.6 17.1 %copy-start = (f32[512,3,32]{0,2,1:T(8,128)S(1)}, f32[512,3,32]{0,2,1:T(8,128)}, u32[]{:S(2)}) copy-start(f32[512,3,32]{0,2,1:T(8,128)} %param.23) | copy-start | bytes 589828
  1.5 3.3 %copy-start.22 = (f32[19,3,1,1]{0,1,3,2:T(4,128)S(1)}, f32[19,3,1,1]{0,1,3,2:T(4,128)}, u32[]{:S(2)}) copy-start(f32[19,3,1,1]{0,1,3,2:T(4,128)} %constant.82) | copy-start | bytes 688
  4.8 1.5 %copy-start.25 = (f32[19]{0:T(128)S(1)}, f32[19]{0:T(128)}, u32[]{:S(2)}) copy-start(f32[19]{0:T(128)} %constant.24.clone) | copy-start | bytes 232
  6.4 1.3 copy-start.3
  7.7 2.8 %copy-start.20 = (f32[6,19,1,1]{1,0,3,2:T(8,128)S(1)}, f32[6,19,1,1]{1,0,3,2:T(8,128)}, u32[]{:S(2)}) copy-start(f32[6,19,1,1]{1,0,3,2:T(8,128)} %constant.83) | copy-start | bytes 1372
  12.8 1.2 copy-start.5
  14.0 3.5 %copy-start.29 = (f32[24,3,32]{2,0,1:T(8,128)S(1)}, f32[24,3,32]{2,0,1:T(8,128)}, u32[]{:S(2)}) copy-start(f32[24,3,32]{2,0,1:T(8,128)} %param.24) | copy-start | bytes 27652
  14.0 36.4 %copy-start.28 = (s32[512]{0:T(512)S(1)}, s32[512]{0:T(512)}, u32[]{:S(2)}) copy-start(s32[512]{0:T(512)} %param.22) | copy-start | bytes 6148
  14.1 87.0 %collective-permute-start.1 = (f32[19,1,64,128]{3,2,1,0:T(8,128)S(1)}, f32[19,1,64,128]{3,2,1,0:T(8,128)}, u32[]{:S(2)}, u32[]{:S(2)}) collective-permute-start(f32[19,1,64,128]{3,2,1,0:T(8,128)S(1)} %slice.827), channel_id=1, source_target_pairs={{1,0},{2,1},{3,2},{4,3},{5,4},{6,5},{7,6},{8,7},{9,8},{10,9},{11,1... | collective-permute-start | bytes 1867784 | tf_op jit(solution)/shard_map/ppermute | solution.py:45
  16.8 60.3 %copy-start.1 = (s32[2,64,128]{2,1,0:T(8,128)S(1)}, s32[2,64,128]{2,1,0:T(8,128)}, u32[]{:S(2)}) copy-start(s32[2,64,128]{2,1,0:T(8,128)} %param.20) | copy-start | bytes 196612
  16.8 60.3 %copy-start.4 = (s32[2,2,64,128]{3,2,1,0:T(8,128)S(1)}, s32[2,2,64,128]{3,2,1,0:T(8,128)}, u32[]{:S(2)}) copy-start(s32[2,2,64,128]{3,2,1,0:T(8,128)} %param.21) | copy-start | bytes 393220
  51.7 25.3 %copy-start.8 = (f32[2,64,128]{2,1,0:T(8,128)S(1)}, f32[2,64,128]{2,1,0:T(8,128)}, u32[]{:S(2)}) copy-start(f32[2,64,128]{2,1,0:T(8,128)} %get-tuple-element.84) | copy-start | bytes 196612
  77.7 1.3 copy-start.12
  83.3 3.4 %copy-start.10 = (f32[2,64,128]{2,1,0:T(8,128)S(1)}, f32[2,64,128]{2,1,0:T(8,128)}, u32[]{:S(2)}) copy-start(f32[2,64,128]{2,1,0:T(8,128)} %copy-done.9) | copy-start | bytes 196612
  83.3 3.4 %copy-start.14 = (f32[2,64,127]{2,1,0:T(8,128)S(1)}, f32[2,64,127]{2,1,0:T(8,128)}, u32[]{:S(2)}) copy-start(f32[2,64,127]{2,1,0:T(8,128)} %slice.815) | copy-start | bytes 195076
  83.3 4.0 %copy-start.13 = (f32[2,64,128]{2,1,0:T(8,128)S(1)}, f32[2,64,128]{2,1,0:T(8,128)}, u32[]{:S(2)}) copy-start(f32[2,64,128]{2,1,0:T(8,128)} %copy-done.12) | copy-start | bytes 196612
  92.9 3.5 %copy-start.2 = (f32[3,8192]{0,1:T(8,128)S(1)}, f32[3,8192]{0,1:T(8,128)}, u32[]{:S(2)}) copy-start(f32[3,8192]{0,1:T(8,128)} %scatter_custom_fusion) | copy-start | bytes 294916
  92.9 3.5 %copy-start.24 = (f32[19,3,1]{0,1,2:T(4,128)S(1)}, f32[19,3,1]{0,1,2:T(4,128)}, u32[]{:S(2)}) copy-start(f32[19,3,1]{0,1,2:T(4,128)} %constant.84) | copy-start | bytes 688
  101.0 7.7 %copy-start.11 = (f32[2,64,128]{2,1,0:T(8,128)S(1)}, f32[2,64,128]{2,1,0:T(8,128)}, u32[]{:S(2)}) copy-start(f32[2,64,128]{2,1,0:T(8,128)} %get-tuple-element.81) | copy-start | bytes 196612
  103.1 13.4 %collective-permute-start = (f32[19,1,64,128]{3,2,1,0:T(8,128)}, f32[19,1,64,128]{3,2,1,0:T(8,128)}, u32[]{:S(2)}, u32[]{:S(2)}) collective-permute-start(f32[19,1,64,128]{3,2,1,0:T(8,128)} %get-tuple-element.80), channel_id=1, source_target_pairs={{0,1},{1,2},{2,3},{3,4},{4,5},{5,6},{6,7},{7,8},{8,9},{9,10},{10,1... | collective-permute-start | bytes 1867784 | tf_op jit(solution)/shard_map/ppermute | solution.py:44
  110.9 5.6 %copy-start.6 = (f32[19,64,128]{2,0,1:T(8,128)S(1)}, f32[19,64,128]{2,0,1:T(8,128)}, u32[]{:S(2)}) copy-start(f32[19,64,128]{2,0,1:T(8,128)} %fusion.172) | copy-start | bytes 1867780
  110.9 5.6 %copy-start.15 = (f32[64,128]{1,0:T(8,128)S(1)}, f32[64,128]{1,0:T(8,128)}, u32[]{:S(2)}) copy-start(f32[64,128]{1,0:T(8,128)} %multiply_bitcast_fusion.3) | copy-start | bytes 98308
  110.9 5.6 %copy-start.26 = (f32[19]{0:T(128)S(1)}, f32[19]{0:T(128)}, u32[]{:S(2)}) copy-start(f32[19]{0:T(128)} %constant.24.clone) | copy-start | bytes 232
  119.2 0.8 copy-start.7
  119.4 0.8 copy-start.19
  120.2 2.0 %copy-start.23 = (f32[19,3,1,1]{0,1,3,2:T(4,128)S(1)}, f32[19,3,1,1]{0,1,3,2:T(4,128)}, u32[]{:S(2)}) copy-start(f32[19,3,1,1]{0,1,3,2:T(4,128)} %constant.82) | copy-start | bytes 688
  126.7 2.5 %copy-start.16 = (pred[2,64,128]{2,1,0:T(8,128)(4,1)S(1)}, pred[2,64,128]{2,1,0:T(8,128)(4,1)}, u32[]{:S(2)}) copy-start(pred[2,64,128]{2,1,0:T(8,128)(4,1)} %get-tuple-element.37) | copy-start | bytes 49156
  126.7 2.7 %copy-start.18 = (pred[2,64,128]{2,1,0:T(8,128)(4,1)S(1)}, pred[2,64,128]{2,1,0:T(8,128)(4,1)}, u32[]{:S(2)}) copy-start(pred[2,64,128]{2,1,0:T(8,128)(4,1)} %get-tuple-element.35) | copy-start | bytes 49156
  126.8 2.7 %copy-start.17 = (pred[2,64,128]{2,1,0:T(8,128)(4,1)S(1)}, pred[2,64,128]{2,1,0:T(8,128)(4,1)}, u32[]{:S(2)}) copy-start(pred[2,64,128]{2,1,0:T(8,128)(4,1)} %get-tuple-element.33) | copy-start | bytes 49156
  126.8 16.1 %collective-permute-start.2 = (f32[19,1,64,128]{3,2,0,1:T(8,128)S(1)}, f32[19,1,64,128]{3,2,0,1:T(8,128)S(1)}, u32[]{:S(2)}, u32[]{:S(2)}) collective-permute-start(f32[19,1,64,128]{3,2,0,1:T(8,128)S(1)} %get-tuple-element.67), channel_id=1, source_target_pairs={{0,1},{1,2},{2,3},{3,4},{4,5},{5,6},{6,7},{7,8},{8,9},{9,10},{10,1... | collective-permute-start | bytes 1867784 | tf_op jit(solution)/shard_map/ppermute | solution.py:44
  129.6 13.7 %collective-permute-start.3 = (f32[19,1,64,128]{3,2,0,1:T(8,128)S(1)}, f32[19,1,64,128]{3,2,0,1:T(8,128)S(1)}, u32[]{:S(2)}, u32[]{:S(2)}) collective-permute-start(f32[19,1,64,128]{3,2,0,1:T(8,128)S(1)} %get-tuple-element.66), channel_id=1, source_target_pairs={{1,0},{2,1},{3,2},{4,3},{5,4},{6,5},{7,6},{8,7},{9,8},{10,9},{11,1... | collective-permute-start | bytes 1867784 | tf_op jit(solution)/shard_map/ppermute | solution.py:45
  145.1 1.0 copy-start.27
  (2 other events, 1.3 us)
where the time goes:
time: 147 us; the launch traced here: 146 us
  blocking collectives  55.3 us (38%)
  other arithmetic  25.1 us (17%)
  matrix products  21.8 us (15%)
  local copies, waits for them, and re-layouts  20 us (14%)
  waiting for transfers between devices  11.2 us (8%)
  starting transfers between devices  10.4 us (7%)
  between operations  2.29 us (2%)
    psum x1, blocking collectives, body(): coefficients = lax.psum(partial_terms, 'ax')  31.4 us
    all_gather x1, blocking collectives, body(): whole_inflow = lax.all_gather(local_inflow, 'ax', axis=2, tiled=True)  23.9 us
    dot_general x4, matrix products, equilibrium(): jnp.einsum('iq,q...->i...', lattice, velocity, precision=lax.Precision.HI...  13.1 us
    ppermute x2, waiting for transfers between devices, extended(): before = lax.ppermute(last, axis, up)  11.2 us
    scatter x2, local copies, waits for them, and re-layouts, inlet_plane(): jnp.zeros((3, height * plane_width), jnp.float32).at[:, inlet_cells]  8.61 us
    reduce_sum x4, other arithmetic, equilibrium(): speed_sq = jnp.sum(velocity * velocity, axis=0)  7.34 us
    ppermute x2, starting transfers between devices, extended(): before = lax.ppermute(last, axis, up)  6.2 us
    dot_general x2, matrix products, collide(): jnp.einsum('mi,i...->m...', moment_rows(), populations, precision=lax.Pre...  4.7 us
  transfers between devices with their start and end apart: 4, of which 1 were waited for; matrix products, arithmetic and copies ran while one was open for 26% of the time, Pallas kernels for 0%

commit v1 on v0

--- a/solution.py
+++ b/solution.py
@@ -1,8 +1,10 @@
+import functools
 import math
 import jax
 import jax.numpy as jnp
 from jax import lax
 from jax.sharding import PartitionSpec as P
+from jax.lax import axis_index, axis_size, ppermute
 
 STEPS = 2
 lattice_c = (
@@ -32,6 +34,29 @@
 relax_base = 0.52
 smagorinsky_sq = 0.04
 inflow_scale = 0.05
+
+
+def bring_the_cubes(block_here, dev_axis):
+    long_array, taken_in, w1 = (axis_size(dev_axis), axis_index(dev_axis), block_here.shape[2])
+    slots = tuple(
+        (p * long_array if hop_no == 2 else p for hop_no, p in enumerate(block_here.shape))
+    )
+    block_next = lax.dynamic_update_slice_in_dim(
+        jnp.zeros(slots, block_here.dtype), block_here, taken_in * w1, axis=2
+    )
+    for h in range(1, long_array):
+        block_here = ppermute(
+            block_here,
+            dev_axis,
+            tuple(((hop_no, (hop_no + 1) % long_array) for hop_no in range(long_array))),
+        )
+        block_next = lax.dynamic_update_slice_in_dim(
+            block_next, block_here, (taken_in - h) % long_array * w1, axis=2
+        )
+    return block_next
+
+
+lead_the_copies = functools.partial(bring_the_cubes, dev_axis="ax")
 
 
 def extended(array, sides, width):
@@ -135,7 +160,7 @@
     local_inflow = jnp.einsum(
         "kjc,sk->sjc", pod_basis, coefficients, precision=lax.Precision.HIGHEST
     )
-    whole_inflow = lax.all_gather(local_inflow, "ax", axis=2, tiled=True)
+    whole_inflow = lead_the_copies(local_inflow)
     position = lax.axis_index("ax")
     axis_count = lax.axis_size("ax")
     height = populations.shape[2]

time: 147 us -> 198 us (1.35)
  waiting for transfers between devices: 11.2 us -> 90.5 us
  blocking collectives: 55.3 us -> 31.5 us
  local copies, waits for them, and re-layouts: 20 us -> 12.6 us
  other arithmetic: 25.1 us -> 28.9 us
  matrix products: 21.8 us -> 19.2 us
  starting transfers between devices: 10.4 us -> 12.5 us
    ppermute x0 -> x15, waiting for transfers between devices: none -> 78.1 us  [bring_the_cubes(): ppermute(block_here, dev_axis, tuple(((hop_no, (hop_no + 1) % long_array)...]
    all_gather x1 -> x0, blocking collectives: 23.9 us -> none  [body(): whole_inflow = lax.all_gather(local_inflow, 'ax', axis=2, tiled=True)]
    scatter x2 -> x0, local copies, waits for them, and re-layouts: 8.61 us -> none  [inlet_plane(): jnp.zeros((3, height * plane_width), jnp.float32).at[:, inlet_cells]]
    scatter x0 -> x2, other arithmetic: none -> 8.13 us  [inlet_plane(): jnp.zeros((3, height * plane_width), jnp.float32).at[:, inlet_cells]]
    dot_general x4, matrix products: 13.1 us -> 10.5 us  [equilibrium(): jnp.einsum('iq,q...->i...', lattice, velocity, precision=lax.Precision.HI...]
    ppermute x0 -> x15, starting transfers between devices: none -> 2.09 us  [bring_the_cubes(): ppermute(block_here, dev_axis, tuple(((hop_no, (hop_no + 1) % long_array)...]
    ppermute x0 -> x15, local copies, waits for them, and re-layouts: none -> 2.04 us  [bring_the_cubes(): ppermute(block_here, dev_axis, tuple(((hop_no, (hop_no + 1) % long_array)...]
    unnamed x61 -> x45, local copies, waits for them, and re-layouts: 4.29 us -> 3.54 us
  transfers between devices with their start and end apart: 4 -> 19, of which waited for: 1 -> 17; matrix products, arithmetic and copies ran while one was open for 26% -> 18% of each run, Pallas kernels for 0% -> 0%
where the time goes in v1:
time: 198 us
  waiting for transfers between devices  90.5 us (46%)
  blocking collectives  31.5 us (16%)
  other arithmetic  28.9 us (15%)
  matrix products  19.2 us (10%)
  local copies, waits for them, and re-layouts  12.6 us (6%)
  starting transfers between devices  12.5 us (6%)
  between operations  2.45 us (1%)
    ppermute x15, waiting for transfers between devices, bring_the_cubes(): ppermute(block_here, dev_axis, tuple(((hop_no, (hop_no + 1) % long_array)...  78.1 us
    psum x1, blocking collectives, body(): coefficients = lax.psum(partial_terms, 'ax')  31.5 us
    ppermute x2, waiting for transfers between devices, extended(): before = lax.ppermute(last, axis, up)  11.6 us
    dot_general x4, matrix products, equilibrium(): jnp.einsum('iq,q...->i...', lattice, velocity, precision=lax.Precision.HI...  10.5 us
    scatter x2, other arithmetic, inlet_plane(): jnp.zeros((3, height * plane_width), jnp.float32).at[:, inlet_cells]  8.13 us
    reduce_sum x4, other arithmetic, equilibrium(): speed_sq = jnp.sum(velocity * velocity, axis=0)  7.3 us
    ppermute x2, starting transfers between devices, extended(): before = lax.ppermute(last, axis, up)  6.53 us
    unnamed x28, other arithmetic  4.96 us
  transfers between devices with their start and end apart: 19, of which 17 were waited for; matrix products, arithmetic and copies ran while one was open for 18% of the time, Pallas kernels for 0%

profile of v1, /device:TPU:1, one launch (start us, length us, event | category | flops | bytes accessed | tf_op | source)
XLA Modules:
  0.0 197.5 jit_solution(1939012870211484256)
XLA Ops:
  0.7 3.0 %fusion.4 = f32[10,2,64,128]{3,0,2,1:T(8,128)S(1)} fusion(f32[10,19,1,1]{1,0,3,2:T(8,128)} %constant.197, f32[19,2,64,128]{3,2,1,0:T(8,128)} %param.19), kind=kOutput, calls=%fused_computation.12 | convolution fusion | flops 37355520 | bytes 1901304 | tf_op jit(solution)/shard_map/mi,i...->m.../dot_general | solution.py:99
  6.8 2.8 %copy_subtract_fusion = f32[19,2,64,128]{3,0,2,1:T(8,128)S(1)} fusion(f32[19,2,64,128]{3,2,1,0:T(8,128)S(1)} %copy-done.4, f32[19,2,64,128]{3,2,1,0:T(8,128)S(1)} %get-tuple-element.98, f32[19,2,64,128]{3,2,1,0:T(8,128)S(1)} %get-tuple-element.61, f32[19,2,64,128]{3,0,2,1:T(8,128)S(1)} %fusion.155, f32[19,2,64,128]{3,2,1,0:T(8,128)S(1)} %get-tuple-element.60, ...), kind=kLoop, calls=%fused_computation.11 | loop fusion | flops 1556480 | bytes 7536640 | tf_op jit(solution)/shard_map/sub | solution.py:104
  14.1 1.9 collective-permute-start.16
  17.1 31.5 %psum.7 = f32[2,512]{1,0:T(2,128)S(1)} all-reduce(f32[2,512]{1,0:T(2,128)S(1)} %convolution_bitcast_fusion), channel_id=1, replica_groups=mesh['case'=2,'ax'=16] {'ax'}, use_global_device_ids=true, to_apply=%region_1.2 | all-reduce | flops 1024 | bytes 8192 | tf_op jit(solution)/shard_map/psum | solution.py:159
  49.6 1.6 collective-permute-start
  60.0 4.1 %collective-permute-done.1 = f32[2,3,32]{2,0,1:T(2,128)S(1)} collective-permute-done((f32[2,3,32]{2,0,1:T(2,128)}, f32[2,3,32]{2,0,1:T(2,128)S(1)}, u32[]{:S(2)}, u32[]{:S(2)}) %collective-permute-start.1) | collective-permute-done | bytes 800 | tf_op jit(solution)/shard_map/ppermute | solution.py:48
  64.2 5.7 %collective-permute-done.2 = f32[2,3,32]{2,0,1:T(2,128)S(1)} collective-permute-done((f32[2,3,32]{2,0,1:T(2,128)S(1)}, f32[2,3,32]{2,0,1:T(2,128)S(1)}, u32[]{:S(2)}, u32[]{:S(2)}) %collective-permute-start.2) | collective-permute-done | bytes 800 | tf_op jit(solution)/shard_map/ppermute | solution.py:48
  70.1 5.7 %collective-permute-done.3 = f32[2,3,32]{2,0,1:T(2,128)S(1)} collective-permute-done((f32[2,3,32]{2,0,1:T(2,128)S(1)}, f32[2,3,32]{2,0,1:T(2,128)S(1)}, u32[]{:S(2)}, u32[]{:S(2)}) %collective-permute-start.3) | collective-permute-done | bytes 800 | tf_op jit(solution)/shard_map/ppermute | solution.py:48
  75.9 5.7 %collective-permute-done.4 = f32[2,3,32]{2,0,1:T(2,128)S(1)} collective-permute-done((f32[2,3,32]{2,0,1:T(2,128)S(1)}, f32[2,3,32]{2,0,1:T(2,128)S(1)}, u32[]{:S(2)}, u32[]{:S(2)}) %collective-permute-start.4) | collective-permute-done | bytes 800 | tf_op jit(solution)/shard_map/ppermute | solution.py:48
  81.9 5.7 %collective-permute-done.5 = f32[2,3,32]{2,0,1:T(2,128)S(1)} collective-permute-done((f32[2,3,32]{2,0,1:T(2,128)S(1)}, f32[2,3,32]{2,0,1:T(2,128)S(1)}, u32[]{:S(2)}, u32[]{:S(2)}) %collective-permute-start.5) | collective-permute-done | bytes 800 | tf_op jit(solution)/shard_map/ppermute | solution.py:48
  87.7 5.7 %collective-permute-done.6 = f32[2,3,32]{2,0,1:T(2,128)S(1)} collective-permute-done((f32[2,3,32]{2,0,1:T(2,128)S(1)}, f32[2,3,32]{2,0,1:T(2,128)S(1)}, u32[]{:S(2)}, u32[]{:S(2)}) %collective-permute-start.6) | collective-permute-done | bytes 800 | tf_op jit(solution)/shard_map/ppermute | solution.py:48
  93.6 5.7 %collective-permute-done.7 = f32[2,3,32]{2,0,1:T(2,128)S(1)} collective-permute-done((f32[2,3,32]{2,0,1:T(2,128)S(1)}, f32[2,3,32]{2,0,1:T(2,128)S(1)}, u32[]{:S(2)}, u32[]{:S(2)}) %collective-permute-start.7) | collective-permute-done | bytes 800 | tf_op jit(solution)/shard_map/ppermute | solution.py:48
  99.4 5.7 %collective-permute-done.8 = f32[2,3,32]{2,0,1:T(2,128)S(1)} collective-permute-done((f32[2,3,32]{2,0,1:T(2,128)S(1)}, f32[2,3,32]{2,0,1:T(2,128)S(1)}, u32[]{:S(2)}, u32[]{:S(2)}) %collective-permute-start.8) | collective-permute-done | bytes 800 | tf_op jit(solution)/shard_map/ppermute | solution.py:48
  105.2 5.7 %collective-permute-done.9 = f32[2,3,32]{2,0,1:T(2,128)S(1)} collective-permute-done((f32[2,3,32]{2,0,1:T(2,128)S(1)}, f32[2,3,32]{2,0,1:T(2,128)S(1)}, u32[]{:S(2)}, u32[]{:S(2)}) %collective-permute-start.9) | collective-permute-done | bytes 800 | tf_op jit(solution)/shard_map/ppermute | solution.py:48
  111.0 5.7 %collective-permute-done.10 = f32[2,3,32]{2,0,1:T(2,128)S(1)} collective-permute-done((f32[2,3,32]{2,0,1:T(2,128)S(1)}, f32[2,3,32]{2,0,1:T(2,128)S(1)}, u32[]{:S(2)}, u32[]{:S(2)}) %collective-permute-start.10) | collective-permute-done | bytes 800 | tf_op jit(solution)/shard_map/ppermute | solution.py:48
  116.9 5.7 %collective-permute-done.11 = f32[2,3,32]{2,0,1:T(2,128)S(1)} collective-permute-done((f32[2,3,32]{2,0,1:T(2,128)S(1)}, f32[2,3,32]{2,0,1:T(2,128)S(1)}, u32[]{:S(2)}, u32[]{:S(2)}) %collective-permute-start.11) | collective-permute-done | bytes 800 | tf_op jit(solution)/shard_map/ppermute | solution.py:48
  122.7 5.7 %collective-permute-done.12 = f32[2,3,32]{2,0,1:T(2,128)S(1)} collective-permute-done((f32[2,3,32]{2,0,1:T(2,128)S(1)}, f32[2,3,32]{2,0,1:T(2,128)S(1)}, u32[]{:S(2)}, u32[]{:S(2)}) %collective-permute-start.12) | collective-permute-done | bytes 800 | tf_op jit(solution)/shard_map/ppermute | solution.py:48
  128.5 5.7 %collective-permute-done.13 = f32[2,3,32]{2,0,1:T(2,128)S(1)} collective-permute-done((f32[2,3,32]{2,0,1:T(2,128)S(1)}, f32[2,3,32]{2,0,1:T(2,128)S(1)}, u32[]{:S(2)}, u32[]{:S(2)}) %collective-permute-start.13) | collective-permute-done | bytes 800 | tf_op jit(solution)/shard_map/ppermute | solution.py:48
  134.4 5.7 %collective-permute-done.14 = f32[2,3,32]{2,0,1:T(2,128)S(1)} collective-permute-done((f32[2,3,32]{2,0,1:T(2,128)S(1)}, f32[2,3,32]{2,0,1:T(2,128)S(1)}, u32[]{:S(2)}, u32[]{:S(2)}) %collective-permute-start.14) | collective-permute-done | bytes 800 | tf_op jit(solution)/shard_map/ppermute | solution.py:48
  140.1 4.1 %scatter_custom_fusion = f32[3,8192]{0,1:T(8,128)} fusion(s32[512]{0:T(512)} %compare_select_fusion, f32[]{:T(128)} %constant.151.clone.1, f32[2,3,512]{1,2,0:T(8,128)S(1)} %constant_dynamic-update-slice_fusion.38, f32[]{:T(128)} %constant.184.clone.1), kind=kCustom, calls=%fused_computation.7 | custom fusion | flops 1536 | bytes 361472 | tf_op jit(solution)/shard_map/scatter | solution.py:140
  144.2 3.3 %multiply_reduce_fusion.1 = f32[8192]{0:T(1024)S(1)} fusion(f32[3,8192]{0,1:T(8,128)} %scatter_custom_fusion), kind=kLoop, calls=%fused_computation.3 | loop fusion | flops 40960 | bytes 131072 | tf_op jit(solution)/shard_map/reduce_sum | solution.py:90
  147.6 4.0 %scatter_custom_fusion.1 = f32[3,8192]{0,1:T(8,128)} fusion(s32[512]{0:T(512)} %compare_select_fusion, f32[]{:T(128)} %constant.151.clone.1, f32[2,3,512]{1,2,0:T(8,128)S(1)} %constant_dynamic-update-slice_fusion.38, f32[]{:T(128)} %constant.184.clone.1), kind=kCustom, calls=%fused_computation.5 | custom fusion | flops 1536 | bytes 361472 | tf_op jit(solution)/shard_map/scatter | solution.py:140
  151.6 3.5 %multiply_reduce_fusion = f32[8192]{0:T(1024)S(1)} fusion(f32[3,8192]{0,1:T(8,128)} %scatter_custom_fusion.1), kind=kLoop, calls=%fused_computation.2 | loop fusion | flops 40960 | bytes 131072 | tf_op jit(solution)/shard_map/reduce_sum | solution.py:90
  155.1 3.7 %fusion.178 = f32[19,64,128]{2,0,1:T(8,128)S(1)} fusion(f32[19,3,1]{0,1,2:T(4,128)S(1)} %copy-done.16, f32[3,64,128]{0,2,1:T(8,128)S(1)} %bitcast.600), kind=kOutput, calls=%fused_computation.363 | convolution fusion | flops 5603328 | bytes 721124 | tf_op jit(solution)/shard_map/iq,q...->i.../dot_general | solution.py:89
  160.1 2.1 %collective-permute-start.15 = (f32[19,1,64,128]{3,2,1,0:T(8,128)S(1)}, f32[19,1,64,128]{3,2,1,0:T(8,128)S(1)}, u32[]{:S(2)}, u32[]{:S(2)}) collective-permute-start(f32[19,1,64,128]{3,2,1,0:T(8,128)S(1)} %get-tuple-element.80), channel_id=1, source_target_pairs={{0,1},{1,2},{2,3},{3,4},{4,5},{5,6},{6,7},{7,8},{8,9},{9,10},{10,1... | collective-permute-start | bytes 1867784 | tf_op jit(solution)/shard_map/ppermute | solution.py:69
  162.3 3.8 %fusion.179 = f32[19,64,128]{2,0,1:T(8,128)S(1)} fusion(f32[19,3,1]{0,1,2:T(4,128)S(1)} %copy-done.16, f32[3,64,128]{0,2,1:T(8,128)S(1)} %bitcast.599), kind=kOutput, calls=%fused_computation.364 | convolution fusion | flops 5603328 | bytes 721124 | tf_op jit(solution)/shard_map/iq,q...->i.../dot_general | solution.py:89
  166.0 3.1 %collective-permute-done.15 = f32[19,1,64,128]{3,2,1,0:T(8,128)S(1)} collective-permute-done((f32[19,1,64,128]{3,2,1,0:T(8,128)S(1)}, f32[19,1,64,128]{3,2,1,0:T(8,128)S(1)}, u32[]{:S(2)}, u32[]{:S(2)}) %collective-permute-start.15) | collective-permute-done | bytes 622624 | tf_op jit(solution)/shard_map/ppermute | solution.py:69
  171.6 1.7 fusion.8
  175.8 1.6 fusion.6
  178.3 4.4 %collective-permute-start.17 = (f32[19,1,64,128]{3,2,0,1:T(8,128)S(1)}, f32[19,1,64,128]{3,2,0,1:T(8,128)S(1)}, u32[]{:S(2)}, u32[]{:S(2)}) collective-permute-start(f32[19,1,64,128]{3,2,0,1:T(8,128)S(1)} %get-tuple-element.67), channel_id=1, source_target_pairs={{0,1},{1,2},{2,3},{3,4},{4,5},{5,6},{6,7},{7,8},{8,9},{9,10},{10,1... | collective-permute-start | bytes 1867784 | tf_op jit(solution)/shard_map/ppermute | solution.py:69
  183.1 1.9 collective-permute-start.18
  185.1 8.5 %collective-permute-done.17 = f32[19,1,64,128]{3,2,0,1:T(8,128)S(1)} collective-permute-done((f32[19,1,64,128]{3,2,0,1:T(8,128)S(1)}, f32[19,1,64,128]{3,2,0,1:T(8,128)S(1)}, u32[]{:S(2)}, u32[]{:S(2)}) %collective-permute-start.17) | collective-permute-done | bytes 622624 | tf_op jit(solution)/shard_map/ppermute | solution.py:69
  (216 shorter events, 30.2 us)
Async XLA Ops:
  0.6 16.2 %copy-start = (f32[512,3,32]{0,2,1:T(8,128)S(1)}, f32[512,3,32]{0,2,1:T(8,128)}, u32[]{:S(2)}) copy-start(f32[512,3,32]{0,2,1:T(8,128)} %param.23) | copy-start | bytes 589828
  0.6 3.3 %copy-start.14 = (f32[19,3,1,1]{0,1,3,2:T(4,128)S(1)}, f32[19,3,1,1]{0,1,3,2:T(4,128)}, u32[]{:S(2)}) copy-start(f32[19,3,1,1]{0,1,3,2:T(4,128)} %constant.198) | copy-start | bytes 688
  13.2 3.5 %copy-start.21 = (f32[24,3,32]{2,0,1:T(8,128)S(1)}, f32[24,3,32]{2,0,1:T(8,128)}, u32[]{:S(2)}) copy-start(f32[24,3,32]{2,0,1:T(8,128)} %param.24) | copy-start | bytes 27652
  13.2 39.6 %copy-start.5 = (s32[2,2,64,128]{3,2,1,0:T(8,128)S(1)}, s32[2,2,64,128]{3,2,1,0:T(8,128)}, u32[]{:S(2)}) copy-start(s32[2,2,64,128]{3,2,1,0:T(8,128)} %param.21) | copy-start | bytes 393220
  14.1 144.8 %collective-permute-start.16 = (f32[19,1,64,128]{3,2,1,0:T(8,128)}, f32[19,1,64,128]{3,2,1,0:T(8,128)}, u32[]{:S(2)}, u32[]{:S(2)}) collective-permute-start(f32[19,1,64,128]{3,2,1,0:T(8,128)} %slice.827), channel_id=1, source_target_pairs={{1,0},{2,1},{3,2},{4,3},{5,4},{6,5},{7,6},{8,7},{9,8},{10,9},{11,1... | collective-permute-start | bytes 1867784 | tf_op jit(solution)/shard_map/ppermute | solution.py:70
  49.6 9.5 %collective-permute-start = (f32[2,3,32]{2,0,1:T(2,128)}, f32[2,3,32]{2,0,1:T(2,128)}, u32[]{:S(2)}, u32[]{:S(2)}) collective-permute-start(f32[2,3,32]{2,0,1:T(2,128)} %fusion.145), channel_id=1, source_target_pairs={{0,1},{1,2},{2,3},{3,4},{4,5},{5,6},{6,7},{7,8},{8,9},{9,10},{10,1... | collective-permute-start | bytes 2312 | tf_op jit(solution)/shard_map/ppermute | solution.py:48
  52.7 3.8 %copy-start.20 = (s32[512]{0:T(512)S(1)}, s32[512]{0:T(512)}, u32[]{:S(2)}) copy-start(s32[512]{0:T(512)} %param.22) | copy-start | bytes 6148
  59.9 4.2 %collective-permute-start.1 = (f32[2,3,32]{2,0,1:T(2,128)}, f32[2,3,32]{2,0,1:T(2,128)S(1)}, u32[]{:S(2)}, u32[]{:S(2)}) collective-permute-start(f32[2,3,32]{2,0,1:T(2,128)} %collective-permute-done), channel_id=1, source_target_pairs={{0,1},{1,2},{2,3},{3,4},{4,5},{5,6},{6,7},{7,8},{8,9},{9,10},{10,1... | collective-permute-start | bytes 2312 | tf_op jit(solution)/shard_map/ppermute | solution.py:48
  64.2 5.8 %collective-permute-start.2 = (f32[2,3,32]{2,0,1:T(2,128)S(1)}, f32[2,3,32]{2,0,1:T(2,128)S(1)}, u32[]{:S(2)}, u32[]{:S(2)}) collective-permute-start(f32[2,3,32]{2,0,1:T(2,128)S(1)} %collective-permute-done.1), channel_id=1, source_target_pairs={{0,1},{1,2},{2,3},{3,4},{4,5},{5,6},{6,7},{7,8},{8,9},{9,10},{10,1... | collective-permute-start | bytes 2312 | tf_op jit(solution)/shard_map/ppermute | solution.py:48
  70.0 5.7 %collective-permute-start.3 = (f32[2,3,32]{2,0,1:T(2,128)S(1)}, f32[2,3,32]{2,0,1:T(2,128)S(1)}, u32[]{:S(2)}, u32[]{:S(2)}) collective-permute-start(f32[2,3,32]{2,0,1:T(2,128)S(1)} %collective-permute-done.2), channel_id=1, source_target_pairs={{0,1},{1,2},{2,3},{3,4},{4,5},{5,6},{6,7},{7,8},{8,9},{9,10},{10,1... | collective-permute-start | bytes 2312 | tf_op jit(solution)/shard_map/ppermute | solution.py:48
  75.9 5.7 %collective-permute-start.4 = (f32[2,3,32]{2,0,1:T(2,128)S(1)}, f32[2,3,32]{2,0,1:T(2,128)S(1)}, u32[]{:S(2)}, u32[]{:S(2)}) collective-permute-start(f32[2,3,32]{2,0,1:T(2,128)S(1)} %collective-permute-done.3), channel_id=1, source_target_pairs={{0,1},{1,2},{2,3},{3,4},{4,5},{5,6},{6,7},{7,8},{8,9},{9,10},{10,1... | collective-permute-start | bytes 2312 | tf_op jit(solution)/shard_map/ppermute | solution.py:48
  81.7 5.9 %collective-permute-start.5 = (f32[2,3,32]{2,0,1:T(2,128)S(1)}, f32[2,3,32]{2,0,1:T(2,128)S(1)}, u32[]{:S(2)}, u32[]{:S(2)}) collective-permute-start(f32[2,3,32]{2,0,1:T(2,128)S(1)} %collective-permute-done.4), channel_id=1, source_target_pairs={{0,1},{1,2},{2,3},{3,4},{4,5},{5,6},{6,7},{7,8},{8,9},{9,10},{10,1... | collective-permute-start | bytes 2312 | tf_op jit(solution)/shard_map/ppermute | solution.py:48
  87.7 5.7 %collective-permute-start.6 = (f32[2,3,32]{2,0,1:T(2,128)S(1)}, f32[2,3,32]{2,0,1:T(2,128)S(1)}, u32[]{:S(2)}, u32[]{:S(2)}) collective-permute-start(f32[2,3,32]{2,0,1:T(2,128)S(1)} %collective-permute-done.5), channel_id=1, source_target_pairs={{0,1},{1,2},{2,3},{3,4},{4,5},{5,6},{6,7},{7,8},{8,9},{9,10},{10,1... | collective-permute-start | bytes 2312 | tf_op jit(solution)/shard_map/ppermute | solution.py:48
  93.5 5.7 %collective-permute-start.7 = (f32[2,3,32]{2,0,1:T(2,128)S(1)}, f32[2,3,32]{2,0,1:T(2,128)S(1)}, u32[]{:S(2)}, u32[]{:S(2)}) collective-permute-start(f32[2,3,32]{2,0,1:T(2,128)S(1)} %collective-permute-done.6), channel_id=1, source_target_pairs={{0,1},{1,2},{2,3},{3,4},{4,5},{5,6},{6,7},{7,8},{8,9},{9,10},{10,1... | collective-permute-start | bytes 2312 | tf_op jit(solution)/shard_map/ppermute | solution.py:48
  99.4 5.7 %collective-permute-start.8 = (f32[2,3,32]{2,0,1:T(2,128)S(1)}, f32[2,3,32]{2,0,1:T(2,128)S(1)}, u32[]{:S(2)}, u32[]{:S(2)}) collective-permute-start(f32[2,3,32]{2,0,1:T(2,128)S(1)} %collective-permute-done.7), channel_id=1, source_target_pairs={{0,1},{1,2},{2,3},{3,4},{4,5},{5,6},{6,7},{7,8},{8,9},{9,10},{10,1... | collective-permute-start | bytes 2312 | tf_op jit(solution)/shard_map/ppermute | solution.py:48
  105.2 5.7 %collective-permute-start.9 = (f32[2,3,32]{2,0,1:T(2,128)S(1)}, f32[2,3,32]{2,0,1:T(2,128)S(1)}, u32[]{:S(2)}, u32[]{:S(2)}) collective-permute-start(f32[2,3,32]{2,0,1:T(2,128)S(1)} %collective-permute-done.8), channel_id=1, source_target_pairs={{0,1},{1,2},{2,3},{3,4},{4,5},{5,6},{6,7},{7,8},{8,9},{9,10},{10,1... | collective-permute-start | bytes 2312 | tf_op jit(solution)/shard_map/ppermute | solution.py:48
  111.0 5.7 %collective-permute-start.10 = (f32[2,3,32]{2,0,1:T(2,128)S(1)}, f32[2,3,32]{2,0,1:T(2,128)S(1)}, u32[]{:S(2)}, u32[]{:S(2)}) collective-permute-start(f32[2,3,32]{2,0,1:T(2,128)S(1)} %collective-permute-done.9), channel_id=1, source_target_pairs={{0,1},{1,2},{2,3},{3,4},{4,5},{5,6},{6,7},{7,8},{8,9},{9,10},{10,1... | collective-permute-start | bytes 2312 | tf_op jit(solution)/shard_map/ppermute | solution.py:48
  116.8 5.7 %collective-permute-start.11 = (f32[2,3,32]{2,0,1:T(2,128)S(1)}, f32[2,3,32]{2,0,1:T(2,128)S(1)}, u32[]{:S(2)}, u32[]{:S(2)}) collective-permute-start(f32[2,3,32]{2,0,1:T(2,128)S(1)} %collective-permute-done.10), channel_id=1, source_target_pairs={{0,1},{1,2},{2,3},{3,4},{4,5},{5,6},{6,7},{7,8},{8,9},{9,10},{10,1... | collective-permute-start | bytes 2312 | tf_op jit(solution)/shard_map/ppermute | solution.py:48
  122.7 5.7 %collective-permute-start.12 = (f32[2,3,32]{2,0,1:T(2,128)S(1)}, f32[2,3,32]{2,0,1:T(2,128)S(1)}, u32[]{:S(2)}, u32[]{:S(2)}) collective-permute-start(f32[2,3,32]{2,0,1:T(2,128)S(1)} %collective-permute-done.11), channel_id=1, source_target_pairs={{0,1},{1,2},{2,3},{3,4},{4,5},{5,6},{6,7},{7,8},{8,9},{9,10},{10,1... | collective-permute-start | bytes 2312 | tf_op jit(solution)/shard_map/ppermute | solution.py:48
  128.5 5.7 %collective-permute-start.13 = (f32[2,3,32]{2,0,1:T(2,128)S(1)}, f32[2,3,32]{2,0,1:T(2,128)S(1)}, u32[]{:S(2)}, u32[]{:S(2)}) collective-permute-start(f32[2,3,32]{2,0,1:T(2,128)S(1)} %collective-permute-done.12), channel_id=1, source_target_pairs={{0,1},{1,2},{2,3},{3,4},{4,5},{5,6},{6,7},{7,8},{8,9},{9,10},{10,1... | collective-permute-start | bytes 2312 | tf_op jit(solution)/shard_map/ppermute | solution.py:48
  134.3 5.7 %collective-permute-start.14 = (f32[2,3,32]{2,0,1:T(2,128)S(1)}, f32[2,3,32]{2,0,1:T(2,128)S(1)}, u32[]{:S(2)}, u32[]{:S(2)}) collective-permute-start(f32[2,3,32]{2,0,1:T(2,128)S(1)} %collective-permute-done.13), channel_id=1, source_target_pairs={{0,1},{1,2},{2,3},{3,4},{4,5},{5,6},{6,7},{7,8},{8,9},{9,10},{10,1... | collective-permute-start | bytes 2312 | tf_op jit(solution)/shard_map/ppermute | solution.py:48
  151.6 3.5 %copy-start.3 = (f32[3,8192]{0,1:T(8,128)S(1)}, f32[3,8192]{0,1:T(8,128)}, u32[]{:S(2)}) copy-start(f32[3,8192]{0,1:T(8,128)} %scatter_custom_fusion) | copy-start | bytes 294916
  151.6 3.5 %copy-start.16 = (f32[19,3,1]{0,1,2:T(4,128)S(1)}, f32[19,3,1]{0,1,2:T(4,128)}, u32[]{:S(2)}) copy-start(f32[19,3,1]{0,1,2:T(4,128)} %constant.200) | copy-start | bytes 688
  155.1 7.1 %copy-start.2 = (f32[3,8192]{0,1:T(8,128)S(1)}, f32[3,8192]{0,1:T(8,128)}, u32[]{:S(2)}) copy-start(f32[3,8192]{0,1:T(8,128)} %scatter_custom_fusion.1) | copy-start | bytes 294916
  160.1 9.1 %collective-permute-start.15 = (f32[19,1,64,128]{3,2,1,0:T(8,128)S(1)}, f32[19,1,64,128]{3,2,1,0:T(8,128)S(1)}, u32[]{:S(2)}, u32[]{:S(2)}) collective-permute-start(f32[19,1,64,128]{3,2,1,0:T(8,128)S(1)} %get-tuple-element.80), channel_id=1, source_target_pairs={{0,1},{1,2},{2,3},{3,4},{4,5},{5,6},{6,7},{7,8},{8,9},{9,10},{10,1... | collective-permute-start | bytes 1867784 | tf_op jit(solution)/shard_map/ppermute | solution.py:69
  162.2 6.9 %copy-start.18 = (f32[19]{0:T(128)S(1)}, f32[19]{0:T(128)}, u32[]{:S(2)}) copy-start(f32[19]{0:T(128)} %constant.191.clone) | copy-start | bytes 232
  178.1 4.6 %copy-start.10 = (pred[2,64,128]{2,1,0:T(8,128)(4,1)S(1)}, pred[2,64,128]{2,1,0:T(8,128)(4,1)}, u32[]{:S(2)}) copy-start(pred[2,64,128]{2,1,0:T(8,128)(4,1)} %get-tuple-element.37) | copy-start | bytes 49156
  178.1 4.8 %copy-start.9 = (pred[2,64,128]{2,1,0:T(8,128)(4,1)S(1)}, pred[2,64,128]{2,1,0:T(8,128)(4,1)}, u32[]{:S(2)}) copy-start(pred[2,64,128]{2,1,0:T(8,128)(4,1)} %get-tuple-element.35) | copy-start | bytes 49156
  178.2 4.8 %copy-start.8 = (pred[2,64,128]{2,1,0:T(8,128)(4,1)S(1)}, pred[2,64,128]{2,1,0:T(8,128)(4,1)}, u32[]{:S(2)}) copy-start(pred[2,64,128]{2,1,0:T(8,128)(4,1)} %get-tuple-element.33) | copy-start | bytes 49156
  178.2 6.8 %copy-start.7 = (pred[2,64,128]{2,1,0:T(8,128)(4,1)S(1)}, pred[2,64,128]{2,1,0:T(8,128)(4,1)}, u32[]{:S(2)}) copy-start(pred[2,64,128]{2,1,0:T(8,128)(4,1)} %get-tuple-element.31) | copy-start | bytes 49156
  178.3 15.3 %collective-permute-start.17 = (f32[19,1,64,128]{3,2,0,1:T(8,128)S(1)}, f32[19,1,64,128]{3,2,0,1:T(8,128)S(1)}, u32[]{:S(2)}, u32[]{:S(2)}) collective-permute-start(f32[19,1,64,128]{3,2,0,1:T(8,128)S(1)} %get-tuple-element.67), channel_id=1, source_target_pairs={{0,1},{1,2},{2,3},{3,4},{4,5},{5,6},{6,7},{7,8},{8,9},{9,10},{10,1... | collective-permute-start | bytes 1867784 | tf_op jit(solution)/shard_map/ppermute | solution.py:69
  183.1 11.6 %collective-permute-start.18 = (f32[19,1,64,128]{3,2,0,1:T(8,128)S(1)}, f32[19,1,64,128]{3,2,0,1:T(8,128)S(1)}, u32[]{:S(2)}, u32[]{:S(2)}) collective-permute-start(f32[19,1,64,128]{3,2,0,1:T(8,128)S(1)} %get-tuple-element.66), channel_id=1, source_target_pairs={{1,0},{2,1},{3,2},{4,3},{5,4},{6,5},{7,6},{8,7},{9,8},{10,9},{11,1... | collective-permute-start | bytes 1867784 | tf_op jit(solution)/shard_map/ppermute | solution.py:70
  (9 other events, 12.3 us)
